TPU v7x, 32 devices: a whole 2x2x4 slice. The times are simulated.
32 devices in a mesh: grp: 2 (over y), sta: 4 (over z), band: 4 (over x, core), src: 1.
Axes of the slice: x: 2, y: 2, z: 4, core: 2. Of those that a mesh axis runs over, the one named last changes fastest.
Arguments:
- spectra: float32 [1, 192, 1024], P('src', ('grp', 'sta', 'band')), parts along dimension 1, may hold values from -6 to 6
- station_place: int32 [192], P('grp'), parts along dimension 0, may hold values from 0 to 95, each once
- tiles: int32 [32, 2], P(('grp', 'sta', 'band')), parts along dimension 0, may hold values from 0 to 1
- observed: float32 [32, 48, 48, 256], P(('grp', 'sta', 'band')), parts along dimension 0, may hold values from -8 to 8
Outputs:
- adjoint: float32 [1, 192, 1024], P('src', ('grp', 'sta', 'band')), parts along dimension 1
There are 2 independent parts, one for each index of `grp`. A program takes and returns all parts, laid end to end along the dimension named above; each array names one. Nothing has to cross between parts.
Inputs may be any that keep to these rules, and one draw needn't show every extreme that they name: station_place is a permutation; block of station s is station_place[s] // 48.
All inputs are finite; a program needn't handle non-finite values.
Results may differ from a plain program's by a relative error of at most 0.00013.
Values sent between devices are 32-bit elements; how exact they have to be, the bound alone decides.
A program may use at most 64 MiB of HBM per device.

v0:
```python
import functools
import math

import jax
import jax.numpy as jnp
import numpy as np
from jax import lax
from jax.experimental import pallas as pl
from jax.experimental.pallas import tpu as pltpu
from jax.sharding import PartitionSpec as P

cubic_weight = 0.1
LANES = 128
MESH = pl.DeviceIdType.MESH


def dft_table(freqs, lags):
    fvals = jnp.arange(freqs, dtype=jnp.float32)
    tvals = jnp.arange(lags, dtype=jnp.float32) - lags // 2
    phase = math.pi / freqs * fvals[:, None] * tvals[None, :]
    return jnp.concatenate([jnp.cos(phase), -jnp.sin(phase)], 0) * (1.0 / math.sqrt(freqs))


def cross_spectrum(left, right):
    half = left.shape[-1] // 2
    lre = left[:, :, None, :half]
    lim = left[:, :, None, half:]
    rre = right[:, None, :, :half]
    rim = right[:, None, :, half:]
    real = jnp.sum(lre * rre + lim * rim, axis=0)
    imag = jnp.sum(lim * rre - lre * rim, axis=0)
    return jnp.concatenate([real, imag], -1)


def adjoint_terms(spectral, left, right):
    half = left.shape[-1] // 2
    are = spectral[:, :, :half]
    aim = spectral[:, :, half:]
    highest = lax.Precision.HIGHEST
    lre, lim = (left[:, :, :half], left[:, :, half:])
    rre, rim = (right[:, :, :half], right[:, :, half:])
    row_re = jnp.einsum("pqf,sqf->spf", are, rre, precision=highest) - jnp.einsum(
        "pqf,sqf->spf", aim, rim, precision=highest
    )
    row_im = jnp.einsum("pqf,sqf->spf", are, rim, precision=highest) + jnp.einsum(
        "pqf,sqf->spf", aim, rre, precision=highest
    )
    col_re = jnp.einsum("pqf,spf->sqf", are, lre, precision=highest) + jnp.einsum(
        "pqf,spf->sqf", aim, lim, precision=highest
    )
    col_im = jnp.einsum("pqf,spf->sqf", are, lim, precision=highest) - jnp.einsum(
        "pqf,spf->sqf", aim, lre, precision=highest
    )
    rows = jnp.concatenate([row_re, row_im], -1)
    cols = jnp.concatenate([col_re, col_im], -1)
    return jnp.concatenate([rows, cols], 1)


def local(spectra, station_place, tiles, observed):
    tile = observed.shape[1]
    lags = observed.shape[3]
    width = spectra.shape[2]
    slots = tiles.shape[0]
    count = station_place.shape[0]
    table = dft_table(width // 2, lags)
    highest = lax.Precision.HIGHEST
    whole = lax.all_gather(spectra[0], ("sta", "band"), axis=0, tiled=True)
    holder = (
        jnp.zeros((count,), jnp.int32).at[station_place].set(jnp.arange(count, dtype=jnp.int32))
    )
    offsets = jnp.arange(tile, dtype=jnp.int32)
    wanted = (tiles[:, :, None] * tile + offsets[None, None, :]).reshape(-1)
    fetched = jnp.take(whole, holder[wanted], axis=0).reshape(slots, 2, tile, width)
    slot = 0
    cross = cross_spectrum(fetched[slot, 0][None], fetched[slot, 1][None]).reshape(
        tile * tile, width
    )
    partial_lags = [jnp.dot(cross, table, precision=highest, preferred_element_type=jnp.float32)]
    lagged = lax.psum(jnp.stack(partial_lags, 0), "src")
    slot = 0
    misfit = lagged[slot] - observed[slot].reshape(tile * tile, lags)
    weighted = misfit + cubic_weight * misfit * misfit * misfit
    spectral = jnp.dot(weighted, table.T, precision=highest, preferred_element_type=jnp.float32)
    terms = adjoint_terms(
        spectral.reshape(tile, tile, width), fetched[slot, 0][None], fetched[slot, 1][None]
    )
    pieces = terms[0]
    select = (station_place[:, None] == wanted[None, :]).astype(jnp.float32)
    mine = lax.psum_scatter(
        jnp.dot(select, pieces, precision=highest, preferred_element_type=jnp.float32),
        ("sta", "band"),
        scatter_dimension=0,
        tiled=True,
    )
    return (mine * (1.0 / tile))[None]

def tables(freqs, lags, lanes):
    fvals = np.arange(freqs, dtype=np.float64)
    tvals = np.arange(lags, dtype=np.float64) - lags // 2
    phase = math.pi / freqs * fvals[:, None] * tvals[None, :]
    scale = 1.0 / math.sqrt(freqs)
    chunks = freqs // lanes
    table = np.stack([np.cos(phase), -np.sin(phase)], 0) * scale
    table = table.reshape(2, chunks, lanes, lags).transpose(1, 0, 2, 3)
    table = table.reshape(chunks, 2 * lanes, lags).astype(np.float32)
    high = table.astype(jnp.bfloat16)
    low = (table - high.astype(np.float32)).astype(jnp.bfloat16)
    down = np.stack([high, low], 0)
    return down, np.ascontiguousarray(down.transpose(0, 1, 3, 2))


def split(value):
    high = value.astype(jnp.bfloat16)
    return high, (value - high.astype(jnp.float32)).astype(jnp.bfloat16)


def mm(a, b):
    return jnp.dot(a, b, preferred_element_type=jnp.float32)


def fused(mesh_sizes, dims, pair_ref, place_ref, spectra_hbm, observed_hbm, down_hbm, up_hbm, out_ref,
          gath, seen, down, up, lag, whigh, wlow, fetched, acc, sendbuf, halfbuf, sumbuf, recvbuf,
          load_sem, table_sem, g1send, g1recv, g2send, g2recv, s1send, s1recv, s2send, s2recv):
    n_sta, n_band = mesh_sizes
    tile, rows, pad, lanes, chunks, block = dims
    n = n_sta * n_band
    pairs = n // 2
    me = lax.axis_index("sta") * n_band + lax.axis_index("band")
    mine, core = me // 2, lax.rem(me, 2)
    real_rows = pl.ds(0, rows)

    def device(pair, side):
        peer = pair * 2 + side
        return {"sta": peer // n_band, "band": lax.rem(peer, n_band)}

    def other(k):
        return lax.rem(mine + k, pairs)

    own = [
        pltpu.make_async_copy(
            spectra_hbm.at[r, pl.ds(h * chunks, chunks), :],
            gath.at[pl.ds(0, chunks), core, mine, r, pl.ds(h * lanes, lanes)],
            load_sem.at[r, h],
        )
        for r in range(rows) for h in range(2)
    ]
    for load in own:
        load.start()
    loads = [
        pltpu.make_async_copy(down_hbm, down, table_sem.at[0]),
        pltpu.make_async_copy(observed_hbm, seen, table_sem.at[1]),
        pltpu.make_async_copy(up_hbm, up, table_sem.at[2]),
    ]
    for load in loads:
        load.start()

    barrier = pltpu.get_barrier_semaphore()

    @pl.loop(1, pairs)
    def _(k):
        pl.semaphore_signal(barrier, inc=1, device_id=device(other(k), core), device_id_type=MESH)

    pl.semaphore_signal(barrier, inc=1, device_id=device(mine, 1 - core), device_id_type=MESH)
    pl.semaphore_wait(barrier, pairs)

    def remote(src, dst, send, recv, pair, side):
        return pltpu.make_async_remote_copy(
            src_ref=src, dst_ref=dst, send_sem=send, recv_sem=recv,
            device_id=device(pair, side), device_id_type=MESH,
        )

    def spread(c, k, holder):
        part = gath.at[c, core, holder, real_rows, :]
        return remote(part, part, g1send.at[c, k], g1recv.at[c, k], other(k), core)

    def forward(c, side):
        part = gath.at[c, side, :, real_rows, :]
        return remote(part, part, g2send.at[c], g2recv.at[c], mine, 1 - core)

    def relay(c):
        @pl.loop(1, pairs)
        def _(k):
            spread(c, k, lax.rem(mine + pairs - k, pairs)).wait_recv()

        forward(c, core).start()

    for load in own:
        load.wait()
    for c in range(chunks):
        @pl.loop(1, pairs)
        def _(k):
            spread(c, k, mine).start()

    count = n * rows
    f32 = jnp.float32
    s_idx = lax.broadcasted_iota(jnp.int32, (count, n * pad), 0)
    g_idx = lax.broadcasted_iota(jnp.int32, (count, n * pad), 1)
    holder = s_idx // rows
    s_row = (holder % 2 * pairs + holder // 2) * pad + s_idx % rows
    expand = (s_row == g_idx).astype(f32)
    places = jnp.broadcast_to(place_ref[...].astype(f32) + 1.0, (8, count))
    places = lax.dot(places, expand, precision=lax.Precision.HIGHEST, preferred_element_type=f32)
    places = jnp.broadcast_to(places[0:1, :], (2 * tile, n * pad))
    j_idx = lax.broadcasted_iota(jnp.int32, (2 * tile, n * pad), 0)
    wanted = jnp.where(j_idx < tile, pair_ref[0, 0] * tile + j_idx, pair_ref[0, 1] * tile + j_idx - tile)
    select32 = (jnp.abs(places - 1.0 - wanted.astype(f32)) < 0.5).astype(f32)
    select = select32.astype(jnp.bfloat16)
    back = jnp.transpose(select32).astype(jnp.bfloat16)
    valid = lax.broadcasted_iota(jnp.int32, (n * pad, 2 * lanes), 0) % pad < rows

    relay(0)
    loads[0].wait()
    steps = tile // block
    span = block * tile
    for c in range(chunks):
        if c + 1 < chunks:
            relay(c + 1)
        forward(c, 1 - core).wait_recv()
        whole = jnp.where(valid, gath[c].reshape(n * pad, 2 * lanes), 0.0)
        high, rest = split(whole)
        low = (whole - high.astype(f32) - rest.astype(f32)).astype(jnp.bfloat16)
        fetched[c] = mm(select, high) + mm(select, rest) + mm(select, low)

        @pl.loop(0, steps, unroll=True)
        def _(b):
            p0 = pl.multiple_of(b * block, block)
            at = pl.ds(pl.multiple_of(b * span, span), span)
            left = fetched[c, pl.ds(p0, block), :]
            lre, lim = left[:, None, :lanes], left[:, None, lanes:]
            right = fetched[c, pl.ds(tile, tile), :]
            rre, rim = right[None, :, :lanes], right[None, :, lanes:]
            real = (lre * rre + lim * rim).reshape(span, lanes)
            imag = (lim * rre - lre * rim).reshape(span, lanes)
            high, low = split(jnp.concatenate([real, imag], -1))
            got = mm(high, down[0, c]) + mm(low, down[0, c]) + mm(high, down[1, c])
            if c > 0:
                got = got + lag[at, :]
            if c < chunks - 1:
                lag[at, :] = got
            else:
                misfit = got - seen[at, :]
                weighted = misfit + cubic_weight * misfit * misfit * misfit
                high, low = split(weighted)
                whigh[at, :] = high
                wlow[at, :] = low

        if c == chunks - 2:
            loads[1].wait()
    loads[2].wait()

    def swap(c):
        return remote(
            sendbuf.at[c, 1 - core, :, real_rows, :], halfbuf.at[c, :, real_rows, :],
            s1send.at[c], s1recv.at[c], mine, 1 - core,
        )

    def deliver(c, k):
        return remote(
            sumbuf.at[c, other(k), real_rows, :], recvbuf.at[c, k, real_rows, :],
            s2send.at[c, k], s2recv.at[c, k], other(k), core,
        )

    def combine(c):
        swap(c).wait_recv()
        sumbuf[c] = sendbuf[c, core] + halfbuf[c]

        @pl.loop(1, pairs)
        def _(k):
            deliver(c, k).start()

    for c in range(chunks):
        acc[pl.ds(tile, tile), :] = jnp.zeros((tile, 2 * lanes), f32)

        @pl.loop(0, steps, unroll=True)
        def _(b):
            p0 = pl.multiple_of(b * block, block)
            at = pl.ds(pl.multiple_of(b * span, span), span)
            high, low = whigh[at, :], wlow[at, :]
            got = mm(high, up[0, c]) + mm(low, up[0, c]) + mm(high, up[1, c])
            got = got.reshape(block, tile, 2 * lanes)
            are, aim = got[:, :, :lanes], got[:, :, lanes:]
            left = fetched[c, pl.ds(p0, block), :]
            lre, lim = left[:, None, :lanes], left[:, None, lanes:]
            right = fetched[c, pl.ds(tile, tile), :]
            rre, rim = right[None, :, :lanes], right[None, :, lanes:]
            acc[pl.ds(p0, block), pl.ds(0, lanes)] = jnp.sum(are * rre - aim * rim, 1)
            acc[pl.ds(p0, block), pl.ds(lanes, lanes)] = jnp.sum(are * rim + aim * rre, 1)
            acc[pl.ds(tile, tile), pl.ds(0, lanes)] += jnp.sum(are * lre + aim * lim, 0)
            acc[pl.ds(tile, tile), pl.ds(lanes, lanes)] += jnp.sum(are * lim - aim * lre, 0)

        high, low = split(acc[...])
        sendbuf[c] = (mm(back, high) + mm(back, low)).reshape(2, pairs, pad, 2 * lanes)
        swap(c).start()
        if c > 0:
            combine(c - 1)
    combine(chunks - 1)

    for c in range(chunks):
        @pl.loop(1, pairs)
        def _(k):
            deliver(c, k).wait_recv()

        total = sumbuf[c, mine]
        for k in range(1, pairs):
            total = total + recvbuf[c, k]
        total = total * (1.0 / tile)
        for h in range(2):
            out_ref[:, h * chunks + c, :] = total[:rows, h * lanes:(h + 1) * lanes]

    for c in range(chunks):
        forward(c, core).wait_send()
        swap(c).wait_send()

        @pl.loop(1, pairs)
        def _(k):
            spread(c, k, mine).wait_send()
            deliver(c, k).wait_send()


def one_kernel(mesh, spectra, station_place, tiles, observed):
    n_sta, n_band = mesh.shape["sta"], mesh.shape["band"]
    n = n_sta * n_band
    tile, lags = observed.shape[1], observed.shape[3]
    rows, width = spectra.shape[1], spectra.shape[2]
    lanes = LANES
    half = width // 2
    chunks = half // lanes
    pad = -(-rows // 8) * 8
    block = 8
    down, up = tables(half, lags, lanes)
    f32, bf16 = jnp.float32, jnp.bfloat16
    dma = pltpu.SemaphoreType.DMA
    anywhere = pl.BlockSpec(memory_space=pl.ANY)
    out = pl.pallas_call(
        functools.partial(fused, (n_sta, n_band), (tile, rows, pad, lanes, chunks, block)),
        out_shape=jax.ShapeDtypeStruct((rows, 2 * chunks, lanes), f32),
        in_specs=[
            pl.BlockSpec(memory_space=pltpu.SMEM), pl.BlockSpec(memory_space=pltpu.VMEM),
            anywhere, anywhere, anywhere, anywhere,
        ],
        out_specs=pl.BlockSpec(memory_space=pltpu.VMEM),
        scratch_shapes=[
            pltpu.VMEM((chunks, 2, n // 2, pad, 2 * lanes), f32),
            pltpu.VMEM((tile * tile, lags), f32),
            pltpu.VMEM(down.shape, bf16),
            pltpu.VMEM(up.shape, bf16),
            pltpu.VMEM((tile * tile, lags), f32),
            pltpu.VMEM((tile * tile, lags), bf16),
            pltpu.VMEM((tile * tile, lags), bf16),
            pltpu.VMEM((chunks, 2 * tile, 2 * lanes), f32),
            pltpu.VMEM((2 * tile, 2 * lanes), f32),
            pltpu.VMEM((chunks, 2, n // 2, pad, 2 * lanes), f32),
            pltpu.VMEM((chunks, n // 2, pad, 2 * lanes), f32),
            pltpu.VMEM((chunks, n // 2, pad, 2 * lanes), f32),
            pltpu.VMEM((chunks, n // 2, pad, 2 * lanes), f32),
            dma((rows, 2)), dma((3,)),
            dma((chunks, n // 2)), dma((chunks, n // 2)), dma((chunks,)), dma((chunks,)),
            dma((chunks,)), dma((chunks,)), dma((chunks, n // 2)), dma((chunks, n // 2)),
        ],
        compiler_params=pltpu.CompilerParams(collective_id=0, has_side_effects=True),
        name="adjoint_kernel",
    )(
        tiles, station_place.reshape(1, -1), spectra.reshape(rows, 2 * chunks, lanes),
        observed.reshape(tile * tile, lags), jnp.asarray(down), jnp.asarray(up),
    )
    return out.reshape(1, rows, width)


def solution(mesh):
    placed = (
        P("src", ("grp", "sta", "band"), None),
        P("grp"),
        P(("grp", "sta", "band"), None),
        P(("grp", "sta", "band"), None, None, None),
    )
    def body(spectra, station_place, tiles, observed):
        fits = (
            mesh.shape["src"] == 1 and mesh.shape["band"] % 2 == 0 and spectra.shape[0] == 1 and tiles.shape[0] == 1
            and spectra.shape[2] % (2 * LANES) == 0 and observed.shape[1] % 8 == 0
        )
        if fits:
            return one_kernel(mesh, spectra, station_place, tiles, observed)
        return local(spectra, station_place, tiles, observed)

    return jax.shard_map(
        body,
        mesh=mesh,
        in_specs=placed,
        out_specs=P("src", ("grp", "sta", "band"), None),
        check_vma=False,
    )
```

profile of v0, /device:TPU:0, one launch (start us, length us, event | category | flops | bytes accessed | tf_op | source)
XLA Modules:
  0.0 33.7 jit_solution(15216870990451046758)
XLA Ops:
  0.0 32.3 %adjoint_kernel.1 = f32[6,8,128]{2,1,0:T(8,128)} custom-call(s32[1,2]{1,0:T(1,128)} %pair_ref.1, s32[1,96]{1,0:T(1,128)} %bitcast.7, f32[6,8,128]{2,1,0:T(8,128)} %bitcast.6, f32[2304,256]{1,0:T(8,128)} %bitcast.4, bf16[2,4,256,256]{3,2,1,0:T(8,128)(2,1)} %constant.4.clone.down_hbm, bf16[2,4,256,256]{3,2,1,0:T(8,128)(2,1)} %constant.5.clone.up_hbm), custom_call_target="tpu_custom_call" | custom-call | tf_op jit(solution)/shard_map/adjoint_kernel/pallas_call | solution.py:334
  32.4 1.3 %copy.10 = f32[1,6,1024]{2,0,1:T(1,128)} copy(f32[1,6,1024]{2,0,1:T(1,128)} %bitcast.5) | data formatting | bytes 49152
where the time goes:
time: 33.9 us; the launch traced here: 33.7 us
  Pallas kernels  32.3 us (95%)
  local copies, waits for them, and re-layouts  1.35 us (4%)
    pallas_call x1, Pallas kernels, one_kernel(): pl.pallas_call(functools.partial(fused, (n_sta, n_band), (tile, rows, pad...  32.3 us
    unnamed x1, local copies, waits for them, and re-layouts  1.35 us

commit v1 on v0

--- a/solution.py
+++ b/solution.py
@@ -96,30 +96,42 @@
 
 def tables(freqs, lags, lanes):
     fvals = np.arange(freqs, dtype=np.float64)
-    tvals = np.arange(lags, dtype=np.float64) - lags // 2
+    tvals = np.arange(lags // 2, dtype=np.float64) + 0.5
     phase = math.pi / freqs * fvals[:, None] * tvals[None, :]
     scale = 1.0 / math.sqrt(freqs)
     chunks = freqs // lanes
-    table = np.stack([np.cos(phase), -np.sin(phase)], 0) * scale
-    table = table.reshape(2, chunks, lanes, lags).transpose(1, 0, 2, 3)
-    table = table.reshape(chunks, 2 * lanes, lags).astype(np.float32)
-    high = table.astype(jnp.bfloat16)
-    low = (table - high.astype(np.float32)).astype(jnp.bfloat16)
-    down = np.stack([high, low], 0)
-    return down, np.ascontiguousarray(down.transpose(0, 1, 3, 2))
-
-
-def split(value):
-    high = value.astype(jnp.bfloat16)
-    return high, (value - high.astype(jnp.float32)).astype(jnp.bfloat16)
-
-
-def mm(a, b):
-    return jnp.dot(a, b, preferred_element_type=jnp.float32)
-
-
-def fused(mesh_sizes, dims, pair_ref, place_ref, spectra_hbm, observed_hbm, down_hbm, up_hbm, out_ref,
-          gath, seen, down, up, lag, whigh, wlow, fetched, acc, sendbuf, halfbuf, sumbuf, recvbuf,
+    table = np.stack([np.cos(phase), np.sin(phase)], 0) * scale
+    table = table.reshape(2, chunks, lanes, lags // 2).transpose(1, 0, 2, 3)
+
+    def halves(part):
+        part = part.astype(np.float32)
+        high = part.astype(jnp.bfloat16)
+        low = (part - high.astype(np.float32)).astype(jnp.bfloat16)
+        return np.concatenate([high, low], -1)
+
+    turn = math.pi / (2 * freqs) * fvals.reshape(chunks, 1, lanes)
+    turn = np.concatenate([np.cos(turn), np.sin(turn)], 1).astype(np.float32)
+    return halves(table), halves(2.0 * table.transpose(0, 1, 3, 2)), turn
+
+
+def residue(value):
+    return value - value.astype(jnp.bfloat16).astype(jnp.float32)
+
+
+def fold(value):
+    total = value[:8]
+    for at in range(8, value.shape[0], 8):
+        total = total + value[at:at + 8]
+    return total
+
+
+def halved(acc, lanes):
+    got = pltpu.matmul_pop(acc)
+    return got[:, :lanes] + got[:, lanes:]
+
+
+def fused(mesh_sizes, dims, pair_ref, place_ref, turn_ref, spectra_hbm, observed_hbm, down_hbm, up_hbm, out_ref,
+          gath, seen, down, up, lag, weights, left, right, rturn, fold_re, fold_im, sendbuf, halfbuf, sumbuf, recvbuf,
           load_sem, table_sem, g1send, g1recv, g2send, g2recv, s1send, s1recv, s2send, s2recv):
     n_sta, n_band = mesh_sizes
     tile, rows, pad, lanes, chunks, block = dims
@@ -193,61 +205,37 @@
 
     count = n * rows
     f32 = jnp.float32
-    s_idx = lax.broadcasted_iota(jnp.int32, (count, n * pad), 0)
-    g_idx = lax.broadcasted_iota(jnp.int32, (count, n * pad), 1)
-    holder = s_idx // rows
-    s_row = (holder % 2 * pairs + holder // 2) * pad + s_idx % rows
-    expand = (s_row == g_idx).astype(f32)
-    places = jnp.broadcast_to(place_ref[...].astype(f32) + 1.0, (8, count))
-    places = lax.dot(places, expand, precision=lax.Precision.HIGHEST, preferred_element_type=f32)
+    g_idx = lax.broadcasted_iota(jnp.int32, (8, n * pad), 1)
+    slot = g_idx // pad
+    holder = slot % pairs * 2 + slot // pairs
+    taken = g_idx % pad
+    source = jnp.minimum(holder * rows + taken, count - 1)
+    places = jnp.concatenate([place_ref[...].astype(f32), jnp.zeros((1, n * pad - count), f32)], -1)
+    places = jnp.take_along_axis(jnp.broadcast_to(places, (8, n * pad)), source, axis=1)
+    places = jnp.where(taken < rows, places, -1.0)
     places = jnp.broadcast_to(places[0:1, :], (2 * tile, n * pad))
     j_idx = lax.broadcasted_iota(jnp.int32, (2 * tile, n * pad), 0)
     wanted = jnp.where(j_idx < tile, pair_ref[0, 0] * tile + j_idx, pair_ref[0, 1] * tile + j_idx - tile)
-    select32 = (jnp.abs(places - 1.0 - wanted.astype(f32)) < 0.5).astype(f32)
-    select = select32.astype(jnp.bfloat16)
-    back = jnp.transpose(select32).astype(jnp.bfloat16)
+    select32 = (jnp.abs(places - wanted.astype(f32)) < 0.5).astype(f32)
+    select = jnp.concatenate([select32, select32], -1).astype(jnp.bfloat16)
+    back = jnp.transpose(jnp.concatenate([select32, jnp.zeros((n * pad - 2 * tile, n * pad), f32)], 0))
+    back = jnp.concatenate([back, back], -1).astype(jnp.bfloat16)
     valid = lax.broadcasted_iota(jnp.int32, (n * pad, 2 * lanes), 0) % pad < rows
+    flip = lanes - 1 - lax.broadcasted_iota(jnp.int32, (tile, lanes), 1)
+    half = lanes
+
+    def rows_of(p):
+        return pl.ds(p * tile, tile)
+
+    loads[1].wait()
+    for p in range(tile):
+        before = jnp.take_along_axis(seen[rows_of(p), :half], flip, axis=1)
+        after = seen[rows_of(p), half:]
+        lag[rows_of(p), :half] = -0.5 * (before + after)
+        lag[rows_of(p), half:] = 0.5 * (after - before)
 
     relay(0)
     loads[0].wait()
-    steps = tile // block
-    span = block * tile
-    for c in range(chunks):
-        if c + 1 < chunks:
-            relay(c + 1)
-        forward(c, 1 - core).wait_recv()
-        whole = jnp.where(valid, gath[c].reshape(n * pad, 2 * lanes), 0.0)
-        high, rest = split(whole)
-        low = (whole - high.astype(f32) - rest.astype(f32)).astype(jnp.bfloat16)
-        fetched[c] = mm(select, high) + mm(select, rest) + mm(select, low)
-
-        @pl.loop(0, steps, unroll=True)
-        def _(b):
-            p0 = pl.multiple_of(b * block, block)
-            at = pl.ds(pl.multiple_of(b * span, span), span)
-            left = fetched[c, pl.ds(p0, block), :]
-            lre, lim = left[:, None, :lanes], left[:, None, lanes:]
-            right = fetched[c, pl.ds(tile, tile), :]
-            rre, rim = right[None, :, :lanes], right[None, :, lanes:]
-            real = (lre * rre + lim * rim).reshape(span, lanes)
-            imag = (lim * rre - lre * rim).reshape(span, lanes)
-            high, low = split(jnp.concatenate([real, imag], -1))
-            got = mm(high, down[0, c]) + mm(low, down[0, c]) + mm(high, down[1, c])
-            if c > 0:
-                got = got + lag[at, :]
-            if c < chunks - 1:
-                lag[at, :] = got
-            else:
-                misfit = got - seen[at, :]
-                weighted = misfit + cubic_weight * misfit * misfit * misfit
-                high, low = split(weighted)
-                whigh[at, :] = high
-                wlow[at, :] = low
-
-        if c == chunks - 2:
-            loads[1].wait()
-    loads[2].wait()
-
     def swap(c):
         return remote(
             sendbuf.at[c, 1 - core, :, real_rows, :], halfbuf.at[c, :, real_rows, :],
@@ -268,32 +256,127 @@
         def _(k):
             deliver(c, k).start()
 
-    for c in range(chunks):
-        acc[pl.ds(tile, tile), :] = jnp.zeros((tile, 2 * lanes), f32)
-
-        @pl.loop(0, steps, unroll=True)
-        def _(b):
-            p0 = pl.multiple_of(b * block, block)
-            at = pl.ds(pl.multiple_of(b * span, span), span)
-            high, low = whigh[at, :], wlow[at, :]
-            got = mm(high, up[0, c]) + mm(low, up[0, c]) + mm(high, up[1, c])
-            got = got.reshape(block, tile, 2 * lanes)
-            are, aim = got[:, :, :lanes], got[:, :, lanes:]
-            left = fetched[c, pl.ds(p0, block), :]
-            lre, lim = left[:, None, :lanes], left[:, None, lanes:]
-            right = fetched[c, pl.ds(tile, tile), :]
-            rre, rim = right[None, :, :lanes], right[None, :, lanes:]
-            acc[pl.ds(p0, block), pl.ds(0, lanes)] = jnp.sum(are * rre - aim * rim, 1)
-            acc[pl.ds(p0, block), pl.ds(lanes, lanes)] = jnp.sum(are * rim + aim * rre, 1)
-            acc[pl.ds(tile, tile), pl.ds(0, lanes)] += jnp.sum(are * lre + aim * lim, 0)
-            acc[pl.ds(tile, tile), pl.ds(lanes, lanes)] += jnp.sum(are * lim - aim * lre, 0)
-
-        high, low = split(acc[...])
-        sendbuf[c] = (mm(back, high) + mm(back, low)).reshape(2, pairs, pad, 2 * lanes)
-        swap(c).start()
-        if c > 0:
-            combine(c - 1)
-    combine(chunks - 1)
+    delay, slots = 8, 10
+
+    def compute(*accs):
+        even, odd, spare, wide = accs[:slots], accs[slots:2 * slots], accs[2 * slots], accs[2 * slots + 1]
+
+        def doubled(part):
+            return jnp.concatenate([part, part], 0)
+
+        def prepare(c):
+            whole = jnp.where(valid, gath[c].reshape(n * pad, 2 * lanes), 0.0)
+            pltpu.matmul_push_rhs(jnp.concatenate([whole, residue(whole)], 0), 0, 0)
+            pltpu.matmul_acc_lhs(spare, select, 0)
+            got = pltpu.matmul_pop(spare)
+            wc, ws = turn_ref[c, 0:1, :], turn_ref[c, 1:2, :]
+            lre, lim, rre, rim = got[:tile, :lanes], got[:tile, lanes:], got[tile:, :lanes], got[tile:, lanes:]
+            lre, lim = lre * wc + lim * ws, lim * wc - lre * ws
+            for k, part in enumerate((lre, lim, lre + lim, lre - lim)):
+                left[c, k] = part
+            tre, tim = rre * wc - rim * ws, rim * wc + rre * ws
+            for k, part in enumerate((tre, tre + tim, tim - tre)):
+                rturn[c, k] = part
+            for k, part in enumerate((rre, rre + rim, rre - rim)):
+                right[k] = part
+
+        def down_step(c, p):
+            row = pl.ds(p, 1)
+            both = right[0] * left[c, 2, row, :]
+            re = both - left[c, 1, row, :] * right[2]
+            im = both - left[c, 0, row, :] * right[1]
+            load = 0 if p == 0 else None
+            pltpu.matmul_acc_lhs(even[p % slots], jnp.concatenate([re, residue(re)], -1), load)
+            pltpu.matmul_acc_lhs(odd[p % slots], jnp.concatenate([im, residue(im)], -1), load)
+
+        def down_end(c, p):
+            at = rows_of(p)
+            e = lag[at, :half] + halved(even[p % slots], lanes)
+            o = lag[at, half:] + halved(odd[p % slots], lanes)
+            if c < chunks - 1:
+                lag[at, :half] = e
+                lag[at, half:] = o
+            else:
+                ee, oo = (2.0 * cubic_weight) * e * e, (2.0 * cubic_weight) * o * o
+                base = 1.5 * (ee + oo) + 1.0
+                for k, part in enumerate((e * (base - ee), o * (base - oo))):
+                    high = part.astype(jnp.bfloat16)
+                    weights[k, at, :lanes] = high
+                    weights[k, at, lanes:] = (part - high.astype(f32)).astype(jnp.bfloat16)
+
+        for c in range(chunks):
+            if c + 1 < chunks:
+                relay(c + 1)
+            forward(c, 1 - core).wait_recv()
+            prepare(c)
+            for k in range(2):
+                pltpu.matmul_push_rhs(doubled(down[c, k]), 0, k)
+            for p in range(tile + delay):
+                if p < tile:
+                    down_step(c, p)
+                if p >= delay:
+                    down_end(c, p - delay)
+
+        loads[2].wait()
+        for c in range(chunks):
+            cols = [None] * 3
+            sums = [None, None]
+
+            def add(at, term):
+                cols[at] = term if cols[at] is None else cols[at] + term
+
+            def up_step(p):
+                load = 0 if p == 0 else None
+                pltpu.matmul_acc_lhs(even[p % slots], weights[0, rows_of(p), :], load)
+                pltpu.matmul_acc_lhs(odd[p % slots], weights[1, rows_of(p), :], load)
+
+            def up_end(p):
+                are = halved(even[p % slots], lanes)
+                aim = halved(odd[p % slots], lanes)
+                row = pl.ds(p, 1)
+                at = pl.ds(p % block * 8, 8)
+                both = are + aim
+                one = fold(both * rturn[c, 0])
+                fold_re[p // block, at, :] = one - fold(aim * rturn[c, 1])
+                fold_im[p // block, at, :] = one + fold(are * rturn[c, 2])
+                add(0, both * left[c, 1, row, :])
+                add(1, are * left[c, 3, row, :])
+                add(2, aim * left[c, 2, row, :])
+
+            for k in range(2):
+                pltpu.matmul_push_rhs(doubled(up[c, k]), 0, k)
+            for p in range(tile + delay):
+                if p < tile:
+                    up_step(p)
+                if p >= delay:
+                    up_end(p - delay)
+            parts = []
+            for part in (fold_re, fold_im):
+                blocks = []
+                for b in range(tile // block):
+                    total = part[b, pl.ds(0, block, stride=8), :]
+                    for j in range(1, 8):
+                        total = total + part[b, pl.ds(j, block, stride=8), :]
+                    blocks.append(total)
+                parts.append(jnp.concatenate(blocks, 0))
+            terms = jnp.concatenate([
+                jnp.concatenate(parts, -1),
+                jnp.concatenate([cols[0] + cols[1], cols[0] - cols[2]], -1),
+                jnp.zeros((n * pad - 2 * tile, 2 * lanes), f32),
+            ], 0)
+            pltpu.matmul_push_rhs(jnp.concatenate([terms, residue(terms)], 0), 0, 0)
+            pltpu.matmul_acc_lhs(wide, back, 0)
+            sendbuf[c] = pltpu.matmul_pop(wide).reshape(2, pairs, pad, 2 * lanes)
+            swap(c).start()
+            if c > 0:
+                combine(c - 1)
+        combine(chunks - 1)
+
+    pl.run_scoped(
+        compute,
+        *[pltpu.ACC(k)((tile, 2 * lanes), f32) for k in (0, 1) for _ in range(slots)],
+        pltpu.ACC(0)((2 * tile, 2 * lanes), f32), pltpu.ACC(0)((n * pad, 2 * lanes), f32),
+    )
 
     for c in range(chunks):
         @pl.loop(1, pairs)
@@ -327,7 +410,7 @@
     chunks = half // lanes
     pad = -(-rows // 8) * 8
     block = 8
-    down, up = tables(half, lags, lanes)
+    down, up, turn = tables(half, lags, lanes)
     f32, bf16 = jnp.float32, jnp.bfloat16
     dma = pltpu.SemaphoreType.DMA
     anywhere = pl.BlockSpec(memory_space=pl.ANY)
@@ -335,7 +418,7 @@
         functools.partial(fused, (n_sta, n_band), (tile, rows, pad, lanes, chunks, block)),
         out_shape=jax.ShapeDtypeStruct((rows, 2 * chunks, lanes), f32),
         in_specs=[
-            pl.BlockSpec(memory_space=pltpu.SMEM), pl.BlockSpec(memory_space=pltpu.VMEM),
+            pl.BlockSpec(memory_space=pltpu.SMEM), pl.BlockSpec(memory_space=pltpu.VMEM), pl.BlockSpec(memory_space=pltpu.VMEM),
             anywhere, anywhere, anywhere, anywhere,
         ],
         out_specs=pl.BlockSpec(memory_space=pltpu.VMEM),
@@ -345,10 +428,12 @@
             pltpu.VMEM(down.shape, bf16),
             pltpu.VMEM(up.shape, bf16),
             pltpu.VMEM((tile * tile, lags), f32),
-            pltpu.VMEM((tile * tile, lags), bf16),
-            pltpu.VMEM((tile * tile, lags), bf16),
-            pltpu.VMEM((chunks, 2 * tile, 2 * lanes), f32),
-            pltpu.VMEM((2 * tile, 2 * lanes), f32),
+            pltpu.VMEM((2, tile * tile, 2 * lanes), bf16),
+            pltpu.VMEM((chunks, 4, tile, lanes), f32),
+            pltpu.VMEM((3, tile, lanes), f32),
+            pltpu.VMEM((chunks, 3, tile, lanes), f32),
+            pltpu.VMEM((tile // block, 8 * block, lanes), f32),
+            pltpu.VMEM((tile // block, 8 * block, lanes), f32),
             pltpu.VMEM((chunks, 2, n // 2, pad, 2 * lanes), f32),
             pltpu.VMEM((chunks, n // 2, pad, 2 * lanes), f32),
             pltpu.VMEM((chunks, n // 2, pad, 2 * lanes), f32),
@@ -360,7 +445,7 @@
         compiler_params=pltpu.CompilerParams(collective_id=0, has_side_effects=True),
         name="adjoint_kernel",
     )(
-        tiles, station_place.reshape(1, -1), spectra.reshape(rows, 2 * chunks, lanes),
+        tiles, station_place.reshape(1, -1), jnp.asarray(turn), spectra.reshape(rows, 2 * chunks, lanes),
         observed.reshape(tile * tile, lags), jnp.asarray(down), jnp.asarray(up),
     )
     return out.reshape(1, rows, width)
@@ -376,7 +461,9 @@
     def body(spectra, station_place, tiles, observed):
         fits = (
             mesh.shape["src"] == 1 and mesh.shape["band"] % 2 == 0 and spectra.shape[0] == 1 and tiles.shape[0] == 1
-            and spectra.shape[2] % (2 * LANES) == 0 and observed.shape[1] % 8 == 0
+            and spectra.shape[2] % (2 * LANES) == 0 and observed.shape[1] % 16 == 0
+            and observed.shape[3] == 2 * LANES and mesh.shape["sta"] * mesh.shape["band"] == 16 and 2 * observed.shape[1] <= LANES
+            and 16 * (-(-spectra.shape[1] // 8) * 8) == LANES
         )
         if fits:
             return one_kernel(mesh, spectra, station_place, tiles, observed)

time: 33.9 us -> 30 us (0.88)
  Pallas kernels: 32.3 us -> 28.4 us
    pallas_call x1, Pallas kernels: 32.3 us -> 28.4 us  [one_kernel(): pl.pallas_call(functools.partial(fused, (n_sta, n_band), (tile, rows, pad...]
where the time goes in v1:
time: 30 us; the launch traced here: 29.8 us
  Pallas kernels  28.4 us (95%)
  local copies, waits for them, and re-layouts  1.35 us (4%)
    pallas_call x1, Pallas kernels, one_kernel(): pl.pallas_call(functools.partial(fused, (n_sta, n_band), (tile, rows, pad...  28.4 us
    unnamed x1, local copies, waits for them, and re-layouts  1.35 us

profile of v1, /device:TPU:0, one launch (start us, length us, event | category | flops | bytes accessed | tf_op | source)
XLA Modules:
  0.0 29.8 jit_solution(14252097841590161635)
XLA Ops:
  0.0 28.4 %adjoint_kernel.1 = f32[6,8,128]{2,1,0:T(8,128)} custom-call(s32[1,2]{1,0:T(1,128)} %pair_ref.1, s32[1,96]{1,0:T(1,128)} %bitcast.7, f32[4,2,128]{2,1,0:T(2,128)} %constant.6.clone.turn_ref, f32[6,8,128]{2,1,0:T(8,128)} %bitcast.6, f32[2304,256]{1,0:T(8,128)} %bitcast.4, bf16[4,2,128,256]{3,2,1,0:T(8,128)(2,1)} %constant.7.clone.down_hbm, ...), custom_call_target="tpu_custom_call" | custom-call | tf_op jit(solution)/shard_map/adjoint_kernel/pallas_call | solution.py:417
  28.4 1.3 %copy.11 = f32[1,6,1024]{2,0,1:T(1,128)} copy(f32[1,6,1024]{2,0,1:T(1,128)} %bitcast.5) | data formatting | bytes 49152

commit v2 on v1

v2 whole, which is shorter than its diff:
```python
import functools
import math

import jax
import jax.numpy as jnp
import numpy as np
from jax import lax
from jax.experimental import pallas as pl
from jax.experimental.pallas import tpu as pltpu
from jax.sharding import PartitionSpec as P

cubic_weight = 0.1
LANES = 128
MESH = pl.DeviceIdType.MESH


def dft_table(freqs, lags):
    fvals = jnp.arange(freqs, dtype=jnp.float32)
    tvals = jnp.arange(lags, dtype=jnp.float32) - lags // 2
    phase = math.pi / freqs * fvals[:, None] * tvals[None, :]
    return jnp.concatenate([jnp.cos(phase), -jnp.sin(phase)], 0) * (1.0 / math.sqrt(freqs))


def cross_spectrum(left, right):
    half = left.shape[-1] // 2
    lre = left[:, :, None, :half]
    lim = left[:, :, None, half:]
    rre = right[:, None, :, :half]
    rim = right[:, None, :, half:]
    real = jnp.sum(lre * rre + lim * rim, axis=0)
    imag = jnp.sum(lim * rre - lre * rim, axis=0)
    return jnp.concatenate([real, imag], -1)


def adjoint_terms(spectral, left, right):
    half = left.shape[-1] // 2
    are = spectral[:, :, :half]
    aim = spectral[:, :, half:]
    highest = lax.Precision.HIGHEST
    lre, lim = (left[:, :, :half], left[:, :, half:])
    rre, rim = (right[:, :, :half], right[:, :, half:])
    row_re = jnp.einsum("pqf,sqf->spf", are, rre, precision=highest) - jnp.einsum(
        "pqf,sqf->spf", aim, rim, precision=highest
    )
    row_im = jnp.einsum("pqf,sqf->spf", are, rim, precision=highest) + jnp.einsum(
        "pqf,sqf->spf", aim, rre, precision=highest
    )
    col_re = jnp.einsum("pqf,spf->sqf", are, lre, precision=highest) + jnp.einsum(
        "pqf,spf->sqf", aim, lim, precision=highest
    )
    col_im = jnp.einsum("pqf,spf->sqf", are, lim, precision=highest) - jnp.einsum(
        "pqf,spf->sqf", aim, lre, precision=highest
    )
    rows = jnp.concatenate([row_re, row_im], -1)
    cols = jnp.concatenate([col_re, col_im], -1)
    return jnp.concatenate([rows, cols], 1)


def local(spectra, station_place, tiles, observed):
    tile = observed.shape[1]
    lags = observed.shape[3]
    width = spectra.shape[2]
    slots = tiles.shape[0]
    count = station_place.shape[0]
    table = dft_table(width // 2, lags)
    highest = lax.Precision.HIGHEST
    whole = lax.all_gather(spectra[0], ("sta", "band"), axis=0, tiled=True)
    holder = (
        jnp.zeros((count,), jnp.int32).at[station_place].set(jnp.arange(count, dtype=jnp.int32))
    )
    offsets = jnp.arange(tile, dtype=jnp.int32)
    wanted = (tiles[:, :, None] * tile + offsets[None, None, :]).reshape(-1)
    fetched = jnp.take(whole, holder[wanted], axis=0).reshape(slots, 2, tile, width)
    slot = 0
    cross = cross_spectrum(fetched[slot, 0][None], fetched[slot, 1][None]).reshape(
        tile * tile, width
    )
    partial_lags = [jnp.dot(cross, table, precision=highest, preferred_element_type=jnp.float32)]
    lagged = lax.psum(jnp.stack(partial_lags, 0), "src")
    slot = 0
    misfit = lagged[slot] - observed[slot].reshape(tile * tile, lags)
    weighted = misfit + cubic_weight * misfit * misfit * misfit
    spectral = jnp.dot(weighted, table.T, precision=highest, preferred_element_type=jnp.float32)
    terms = adjoint_terms(
        spectral.reshape(tile, tile, width), fetched[slot, 0][None], fetched[slot, 1][None]
    )
    pieces = terms[0]
    select = (station_place[:, None] == wanted[None, :]).astype(jnp.float32)
    mine = lax.psum_scatter(
        jnp.dot(select, pieces, precision=highest, preferred_element_type=jnp.float32),
        ("sta", "band"),
        scatter_dimension=0,
        tiled=True,
    )
    return (mine * (1.0 / tile))[None]

def tables(freqs, lags, lanes):
    fvals = np.arange(freqs, dtype=np.float64)
    tvals = np.arange(lags // 2, dtype=np.float64) + 0.5
    phase = math.pi / freqs * fvals[:, None] * tvals[None, :]
    scale = 1.0 / math.sqrt(freqs)
    chunks = freqs // lanes
    table = np.stack([np.cos(phase), np.sin(phase)], 0) * scale
    table = table.reshape(2, chunks, lanes, lags // 2).transpose(1, 0, 2, 3)

    def halves(part):
        part = part.astype(np.float32)
        high = part.astype(jnp.bfloat16)
        low = (part - high.astype(np.float32)).astype(jnp.bfloat16)
        return np.concatenate([high, low], -1)

    turn = math.pi / (2 * freqs) * fvals.reshape(chunks, 1, lanes)
    turn = np.concatenate([np.cos(turn), np.sin(turn)], 1).astype(np.float32)
    return halves(table), halves(2.0 * table.transpose(0, 1, 3, 2)), turn


def residue(value):
    return value - value.astype(jnp.bfloat16).astype(jnp.float32)


def fold(value):
    total = value[:8]
    for at in range(8, value.shape[0], 8):
        total = total + value[at:at + 8]
    return total


def halved(acc, lanes):
    got = pltpu.matmul_pop(acc)
    return got[:, :lanes] + got[:, lanes:]


def fused(mesh_sizes, dims, pair_hbm, place_hbm, turn_hbm, spectra_hbm, observed_hbm, down_hbm, up_hbm, out_ref,
          pair_ref, place_ref, turn_ref, own, gath, seen, down, up, lag, weights, left, right, rturn, fold_re, fold_im,
          terms, sendbuf, halfbuf, sumbuf, recvbuf,
          load_sem, table_sem, g1send, g1recv, g2send, g2recv, s1send, s1recv, s2send, s2recv):
    n_sta, n_band = mesh_sizes
    tile, rows, pad, lanes, chunks, block = dims
    n = n_sta * n_band
    pairs = n // 2
    me = lax.axis_index("sta") * n_band + lax.axis_index("band")
    mine, core = me // 2, lax.rem(me, 2)
    across = 1 - core
    real_rows = pl.ds(0, rows)
    count = n * rows
    f32 = jnp.float32

    def device(pair, side):
        peer = pair * 2 + side
        return {"sta": peer // n_band, "band": lax.rem(peer, n_band)}

    def other(k):
        return lax.rem(mine + k, pairs)

    barrier = pltpu.get_barrier_semaphore()

    @pl.loop(0, pairs)
    def _(k):
        pl.semaphore_signal(barrier, inc=1, device_id=device(other(k), across), device_id_type=MESH)

    own_loads = [
        pltpu.make_async_copy(
            spectra_hbm.at[:, h * chunks + c, :], own.at[c, real_rows, pl.ds(h * lanes, lanes)], load_sem.at[c, h],
        )
        for c in range(chunks) for h in range(2)
    ]
    for load in own_loads:
        load.start()
    loads = [
        pltpu.make_async_copy(src, dst, table_sem.at[at])
        for at, (src, dst) in enumerate((
            (pair_hbm, pair_ref), (place_hbm, place_ref), (observed_hbm, seen),
            (turn_hbm, turn_ref), (down_hbm, down), (up_hbm, up),
        ))
    ]
    for load in loads:
        load.start()

    def remote(src, dst, send, recv, pair, side):
        return pltpu.make_async_remote_copy(
            src_ref=src, dst_ref=dst, send_sem=send, recv_sem=recv,
            device_id=device(pair, side), device_id_type=MESH,
        )

    def spread(c, k):
        return remote(
            own.at[c, real_rows, :], gath.at[c, core, mine, real_rows, :],
            g1send.at[c], g1recv.at[c], other(k), across,
        )

    def arrived(c):
        part = gath.at[c, across, :, real_rows, :]
        return remote(part, part, g1send.at[c], g1recv.at[c], mine, across)

    def forward(c, side):
        part = gath.at[c, side, :, real_rows, :]
        return remote(part, part, g2send.at[c], g2recv.at[c], mine, across)

    def relay(c):
        arrived(c).wait_recv()
        forward(c, across).start()

    def swap(c):
        return remote(
            sendbuf.at[c, core, :, real_rows, :], halfbuf.at[c, :, real_rows, :],
            s1send.at[c], s1recv.at[c], mine, across,
        )

    def deliver(c, k):
        return remote(
            sumbuf.at[c, other(k), real_rows, :], recvbuf.at[c, k, real_rows, :],
            s2send.at[c], s2recv.at[c], other(k), across,
        )

    def delivered(c):
        part = recvbuf.at[c, :, real_rows, :]
        return remote(part, part, s2send.at[c], s2recv.at[c], mine, across)

    def combine(c):
        swap(c).wait_recv()
        sumbuf[c] = sendbuf[c, across] + halfbuf[c]

        @pl.loop(0, pairs)
        def _(k):
            deliver(c, k).start()

    for load in own_loads:
        load.wait()
    pl.semaphore_wait(barrier, pairs)
    for c in range(chunks):
        @pl.loop(0, pairs)
        def _(k):
            spread(c, k).start()

    for load in loads[:2]:
        load.wait()
    g_idx = lax.broadcasted_iota(jnp.int32, (8, n * pad), 1)
    slot = g_idx // pad
    holder = slot % pairs * 2 + slot // pairs
    taken = g_idx % pad
    source = jnp.minimum(holder * rows + taken, count - 1)
    places = jnp.concatenate([place_ref[...].astype(f32), jnp.zeros((1, n * pad - count), f32)], -1)
    places = jnp.take_along_axis(jnp.broadcast_to(places, (8, n * pad)), source, axis=1)
    places = jnp.where(taken < rows, places, -1.0)
    places = jnp.broadcast_to(places[0:1, :], (2 * tile, n * pad))
    j_idx = lax.broadcasted_iota(jnp.int32, (2 * tile, n * pad), 0)
    wanted = jnp.where(j_idx < tile, pair_ref[0, 0] * tile + j_idx, pair_ref[0, 1] * tile + j_idx - tile)
    select32 = (jnp.abs(places - wanted.astype(f32)) < 0.5).astype(f32)
    select = jnp.concatenate([select32, select32], -1).astype(jnp.bfloat16)
    back = jnp.transpose(jnp.concatenate([select32, jnp.zeros((n * pad - 2 * tile, n * pad), f32)], 0))
    back = jnp.concatenate([back, back], -1).astype(jnp.bfloat16)
    valid = lax.broadcasted_iota(jnp.int32, (n * pad, 2 * lanes), 0) % pad < rows
    flip = lanes - 1 - lax.broadcasted_iota(jnp.int32, (tile, lanes), 1)
    terms[pl.ds(2 * tile, n * pad - 2 * tile), :] = jnp.zeros((n * pad - 2 * tile, 2 * lanes), f32)

    def rows_of(p):
        return pl.ds(p * tile, tile)

    loads[2].wait()
    for p in range(tile):
        before = jnp.take_along_axis(seen[rows_of(p), :lanes], flip, axis=1)
        after = seen[rows_of(p), lanes:]
        lag[rows_of(p), :lanes] = -0.5 * (before + after)
        lag[rows_of(p), lanes:] = 0.5 * (after - before)

    for load in loads[3:]:
        load.wait()
    relay(0)
    delay, slots = 8, 10
    steps = chunks * tile

    def compute(*accs):
        accs, spare, wide = (accs[:slots], accs[slots:2 * slots]), accs[2 * slots], accs[2 * slots + 1]
        fresh = [False, False]

        def stage(unit, value):
            pltpu.matmul_push_rhs(value, 0, unit)
            fresh[unit] = True

        def feed(acc, value, unit):
            pltpu.matmul_acc_lhs(acc, value, 0 if fresh[unit] else None)
            fresh[unit] = False

        def table(ref, c, unit):
            part = ref[c, unit]
            stage(unit, jnp.concatenate([part, part], 0))

        def choose(c):
            forward(c, core).wait_recv()
            whole = jnp.where(valid, gath[c].reshape(n * pad, 2 * lanes), 0.0)
            stage(0, jnp.concatenate([whole, residue(whole)], 0))
            feed(spare, select, 0)

        def prepare(c):
            got = pltpu.matmul_pop(spare)
            wc, ws = turn_ref[c, 0:1, :], turn_ref[c, 1:2, :]
            lre, lim, rre, rim = got[:tile, :lanes], got[:tile, lanes:], got[tile:, :lanes], got[tile:, lanes:]
            lre, lim = lre * wc + lim * ws, lim * wc - lre * ws
            for k, part in enumerate((lre, lim, lre + lim, lre - lim)):
                left[c, k] = part
            tre, tim = rre * wc - rim * ws, rim * wc + rre * ws
            for k, part in enumerate((tre, tre + tim, tim - tre)):
                rturn[c, k] = part
            for k, part in enumerate((rre, rre + rim, rre - rim)):
                right[c % 2, k] = part

        def down_step(i):
            c, p = divmod(i, tile)
            row = pl.ds(p, 1)
            if p == 0:
                for unit in range(2):
                    table(down, c, unit)
            both = right[c % 2, 0] * left[c, 2, row, :]
            re = both - left[c, 1, row, :] * right[c % 2, 2]
            im = both - left[c, 0, row, :] * right[c % 2, 1]
            feed(accs[0][i % slots], jnp.concatenate([re, residue(re)], -1), 0)
            feed(accs[1][i % slots], jnp.concatenate([im, residue(im)], -1), 1)

        def down_end(i):
            c, p = divmod(i, tile)
            at = rows_of(p)
            e = lag[at, :lanes] + halved(accs[0][i % slots], lanes)
            o = lag[at, lanes:] + halved(accs[1][i % slots], lanes)
            if c < chunks - 1:
                lag[at, :lanes] = e
                lag[at, lanes:] = o
            else:
                ee, oo = (2.0 * cubic_weight) * e * e, (2.0 * cubic_weight) * o * o
                base = 1.5 * (ee + oo) + 1.0
                for k, part in enumerate((e * (base - ee), o * (base - oo))):
                    weights[k, at, :lanes] = part
                    weights[k, at, lanes:] = residue(part)

        def run(step, end, hooks):
            for i in range(steps + delay):
                for hook in hooks.pop(i, ()):
                    hook()
                if i < steps:
                    step(i)
                if i >= delay:
                    end(i - delay)
            for i in sorted(hooks):
                for hook in hooks[i]:
                    hook()

        choose(0)
        prepare(0)
        relay(1)
        hooks = {}
        for c in range(1, chunks):
            if c > 1:
                hooks.setdefault((c - 2) * tile + 28, []).append(functools.partial(relay, c))
            hooks.setdefault((c - 1) * tile + 32, []).extend(
                [functools.partial(choose, c), functools.partial(table, down, c - 1, 0)]
            )
            hooks.setdefault((c - 1) * tile + 40, []).append(functools.partial(prepare, c))
        run(down_step, down_end, hooks)

        cols = [None] * 3

        def add(at, term):
            cols[at] = term if cols[at] is None else cols[at] + term

        def up_step(i):
            c, p = divmod(i, tile)
            if p == 0:
                for unit in range(2):
                    table(up, c, unit)
            for unit in range(2):
                feed(accs[unit][i % slots], weights[unit, rows_of(p), :], unit)

        def up_end(i):
            c, p = divmod(i, tile)
            are, aim = [halved(accs[unit][i % slots], lanes) for unit in range(2)]
            row = pl.ds(p, 1)
            at = pl.ds(p % block * 8, 8)
            both = are + aim
            one = fold(both * rturn[c, 0])
            fold_re[p // block, at, :] = one - fold(aim * rturn[c, 1])
            fold_im[p // block, at, :] = one + fold(are * rturn[c, 2])
            add(0, both * left[c, 1, row, :])
            add(1, are * left[c, 3, row, :])
            add(2, aim * left[c, 2, row, :])
            if p % block == block - 1:
                for h, part in enumerate((fold_re, fold_im)):
                    total = part[p // block, pl.ds(0, block, stride=8), :]
                    for j in range(1, 8):
                        total = total + part[p // block, pl.ds(j, block, stride=8), :]
                    terms[pl.ds(p + 1 - block, block), pl.ds(h * lanes, lanes)] = total
            if p == tile - 1:
                terms[pl.ds(tile, tile), :lanes] = cols[0] + cols[1]
                terms[pl.ds(tile, tile), lanes:] = cols[0] - cols[2]
                cols[:] = [None] * 3

        def place(c):
            whole = terms[...]
            stage(0, jnp.concatenate([whole, residue(whole)], 0))
            feed(wide, back, 0)
            if c + 1 < chunks:
                table(up, c + 1, 0)

        def send(c):
            sendbuf[c] = pltpu.matmul_pop(wide).reshape(2, pairs, pad, 2 * lanes)
            swap(c).start()

        hooks = {}
        for c in range(chunks):
            at = (c + 1) * tile + delay
            hooks.setdefault(at, []).append(functools.partial(place, c))
            hooks.setdefault(at + 8, []).append(functools.partial(send, c))
            hooks.setdefault(at + 80, []).append(functools.partial(combine, c))
        run(up_step, up_end, hooks)

    pl.run_scoped(
        compute,
        *[pltpu.ACC(k)((tile, 2 * lanes), f32) for k in (0, 1) for _ in range(slots)],
        pltpu.ACC(0)((2 * tile, 2 * lanes), f32), pltpu.ACC(0)((n * pad, 2 * lanes), f32),
    )

    for c in range(chunks):
        delivered(c).wait_recv()
        total = recvbuf[c, 0]
        for k in range(1, pairs):
            total = total + recvbuf[c, k]
        total = total * (1.0 / tile)
        for h in range(2):
            out_ref[:, h * chunks + c, :] = total[:rows, h * lanes:(h + 1) * lanes]

    for c in range(chunks):
        arrived(c).wait_send()
        forward(c, across).wait_send()
        swap(c).wait_send()
        delivered(c).wait_send()


def one_kernel(mesh, spectra, station_place, tiles, observed):
    n_sta, n_band = mesh.shape["sta"], mesh.shape["band"]
    n = n_sta * n_band
    tile, lags = observed.shape[1], observed.shape[3]
    rows, width = spectra.shape[1], spectra.shape[2]
    lanes = LANES
    half = width // 2
    chunks = half // lanes
    pad = -(-rows // 8) * 8
    block = 8
    down, up, turn = tables(half, lags, lanes)
    f32, bf16 = jnp.float32, jnp.bfloat16
    dma = pltpu.SemaphoreType.DMA
    anywhere = pl.BlockSpec(memory_space=pltpu.HBM)
    out = pl.pallas_call(
        functools.partial(fused, (n_sta, n_band), (tile, rows, pad, lanes, chunks, block)),
        out_shape=jax.ShapeDtypeStruct((rows, 2 * chunks, lanes), f32),
        in_specs=[
            anywhere, anywhere, anywhere, anywhere, anywhere, anywhere, anywhere,
        ],
        out_specs=pl.BlockSpec(memory_space=pltpu.VMEM),
        scratch_shapes=[
            pltpu.SMEM((1, 2), jnp.int32),
            pltpu.VMEM((1, n * rows), jnp.int32),
            pltpu.VMEM(turn.shape, f32),
            pltpu.VMEM((chunks, pad, 2 * lanes), f32),
            pltpu.VMEM((chunks, 2, n // 2, pad, 2 * lanes), f32),
            pltpu.VMEM((tile * tile, lags), f32),
            pltpu.VMEM(down.shape, bf16),
            pltpu.VMEM(up.shape, bf16),
            pltpu.VMEM((tile * tile, lags), f32),
            pltpu.VMEM((2, tile * tile, 2 * lanes), f32),
            pltpu.VMEM((chunks, 4, tile, lanes), f32),
            pltpu.VMEM((2, 3, tile, lanes), f32),
            pltpu.VMEM((chunks, 3, tile, lanes), f32),
            pltpu.VMEM((tile // block, 8 * block, lanes), f32),
            pltpu.VMEM((tile // block, 8 * block, lanes), f32),
            pltpu.VMEM((n * pad, 2 * lanes), f32),
            pltpu.VMEM((chunks, 2, n // 2, pad, 2 * lanes), f32),
            pltpu.VMEM((chunks, n // 2, pad, 2 * lanes), f32),
            pltpu.VMEM((chunks, n // 2, pad, 2 * lanes), f32),
            pltpu.VMEM((chunks, n // 2, pad, 2 * lanes), f32),
            dma((chunks, 2)), dma((6,)), dma((chunks,)), dma((chunks,)), dma((chunks,)), dma((chunks,)),
            dma((chunks,)), dma((chunks,)), dma((chunks,)), dma((chunks,)),
        ],
        compiler_params=pltpu.CompilerParams(collective_id=0, has_side_effects=True),
        name="adjoint_kernel",
    )(
        tiles, station_place.reshape(1, -1), jnp.asarray(turn), spectra.reshape(rows, 2 * chunks, lanes),
        observed.reshape(tile * tile, lags), jnp.asarray(down), jnp.asarray(up),
    )
    return out.reshape(1, rows, width)


def solution(mesh):
    placed = (
        P("src", ("grp", "sta", "band"), None),
        P("grp"),
        P(("grp", "sta", "band"), None),
        P(("grp", "sta", "band"), None, None, None),
    )
    def body(spectra, station_place, tiles, observed):
        fits = (
            mesh.shape["src"] == 1 and mesh.shape["band"] % 2 == 0 and spectra.shape[0] == 1 and tiles.shape[0] == 1
            and spectra.shape[2] % (2 * LANES) == 0 and observed.shape[1] % 16 == 0
            and observed.shape[3] == 2 * LANES and mesh.shape["sta"] * mesh.shape["band"] == 16 and 2 * observed.shape[1] <= LANES
            and 16 * (-(-spectra.shape[1] // 8) * 8) == LANES
        )
        if fits:
            return one_kernel(mesh, spectra, station_place, tiles, observed)
        return local(spectra, station_place, tiles, observed)

    return jax.shard_map(
        body,
        mesh=mesh,
        in_specs=placed,
        out_specs=P("src", ("grp", "sta", "band"), None),
        check_vma=False,
    )
```

time: 30 us -> 27.3 us (0.910)
  Pallas kernels: 28.4 us -> 25.6 us
    pallas_call x1, Pallas kernels: 28.4 us -> 25.6 us  [one_kernel(): pl.pallas_call(functools.partial(fused, (n_sta, n_band), (tile, rows, pad...]
where the time goes in v2:
time: 27.3 us; the launch traced here: 27 us
  Pallas kernels  25.6 us (94%)
  local copies, waits for them, and re-layouts  1.35 us (5%)
    pallas_call x1, Pallas kernels, one_kernel(): pl.pallas_call(functools.partial(fused, (n_sta, n_band), (tile, rows, pad...  25.6 us
    unnamed x1, local copies, waits for them, and re-layouts  1.35 us

profile of v2, /device:TPU:0, one launch (start us, length us, event | category | flops | bytes accessed | tf_op | source)
XLA Modules:
  0.0 27.0 jit_solution(16134034086546947853)
XLA Ops:
  0.0 25.6 %adjoint_kernel.1 = f32[6,8,128]{2,1,0:T(8,128)} custom-call(s32[1,2]{1,0:T(1,128)} %pair_hbm.1, s32[1,96]{1,0:T(1,128)} %bitcast.7, f32[4,2,128]{2,1,0:T(2,128)} %constant.6.clone.turn_hbm, f32[6,8,128]{2,1,0:T(8,128)} %bitcast.6, f32[2304,256]{1,0:T(8,128)} %bitcast.4, bf16[4,2,128,256]{3,2,1,0:T(8,128)(2,1)} %constant.7.clone.down_hbm, ...), custom_call_target="tpu_custom_call" | custom-call | tf_op jit(solution)/shard_map/adjoint_kernel/pallas_call | solution.py:450
  25.6 1.3 %copy.11 = f32[1,6,1024]{2,0,1:T(1,128)} copy(f32[1,6,1024]{2,0,1:T(1,128)} %bitcast.5) | data formatting | bytes 49152

commit v3 on v2

--- a/solution.py
+++ b/solution.py
@@ -99,6 +99,7 @@
     tvals = np.arange(lags // 2, dtype=np.float64) + 0.5
     phase = math.pi / freqs * fvals[:, None] * tvals[None, :]
     scale = 1.0 / math.sqrt(freqs)
+    bend = math.sqrt(2.0 * cubic_weight)
     chunks = freqs // lanes
     table = np.stack([np.cos(phase), np.sin(phase)], 0) * scale
     table = table.reshape(2, chunks, lanes, lags // 2).transpose(1, 0, 2, 3)
@@ -111,7 +112,7 @@
 
     turn = math.pi / (2 * freqs) * fvals.reshape(chunks, 1, lanes)
     turn = np.concatenate([np.cos(turn), np.sin(turn)], 1).astype(np.float32)
-    return halves(table), halves(2.0 * table.transpose(0, 1, 3, 2)), turn
+    return halves(bend * table), halves(2.0 / bend * table.transpose(0, 1, 3, 2)), turn
 
 
 def residue(value):
@@ -144,6 +145,7 @@
     real_rows = pl.ds(0, rows)
     count = n * rows
     f32 = jnp.float32
+    bend = math.sqrt(2.0 * cubic_weight)
 
     def device(pair, side):
         peer = pair * 2 + side
@@ -220,9 +222,9 @@
         swap(c).wait_recv()
         sumbuf[c] = sendbuf[c, across] + halfbuf[c]
 
-        @pl.loop(0, pairs)
+        @pl.loop(1, pairs + 1)
         def _(k):
-            deliver(c, k).start()
+            deliver(c, lax.rem(k, pairs)).start()
 
     for load in own_loads:
         load.wait()
@@ -230,7 +232,7 @@
     for c in range(chunks):
         @pl.loop(0, pairs)
         def _(k):
-            spread(c, k).start()
+            spread(c, pairs - 1 - k).start()
 
     for load in loads[:2]:
         load.wait()
@@ -254,19 +256,20 @@
     terms[pl.ds(2 * tile, n * pad - 2 * tile), :] = jnp.zeros((n * pad - 2 * tile, 2 * lanes), f32)
 
     def rows_of(p):
-        return pl.ds(p * tile, tile)
+        return pl.ds(pl.multiple_of(p * tile, 8), tile)
 
     loads[2].wait()
-    for p in range(tile):
+    @pl.loop(0, tile, unroll=4)
+    def _(p):
         before = jnp.take_along_axis(seen[rows_of(p), :lanes], flip, axis=1)
         after = seen[rows_of(p), lanes:]
-        lag[rows_of(p), :lanes] = -0.5 * (before + after)
-        lag[rows_of(p), lanes:] = 0.5 * (after - before)
+        lag[rows_of(p), :lanes] = -0.5 * bend * (before + after)
+        lag[rows_of(p), lanes:] = 0.5 * bend * (after - before)
 
     for load in loads[3:]:
         load.wait()
     relay(0)
-    delay, slots = 8, 10
+    delay, slots = 9, 12
     steps = chunks * tile
 
     def compute(*accs):
@@ -325,7 +328,7 @@
                 lag[at, :lanes] = e
                 lag[at, lanes:] = o
             else:
-                ee, oo = (2.0 * cubic_weight) * e * e, (2.0 * cubic_weight) * o * o
+                ee, oo = e * e, o * o
                 base = 1.5 * (ee + oo) + 1.0
                 for k, part in enumerate((e * (base - ee), o * (base - oo))):
                     weights[k, at, :lanes] = part
@@ -449,7 +452,7 @@
     anywhere = pl.BlockSpec(memory_space=pltpu.HBM)
     out = pl.pallas_call(
         functools.partial(fused, (n_sta, n_band), (tile, rows, pad, lanes, chunks, block)),
-        out_shape=jax.ShapeDtypeStruct((rows, 2 * chunks, lanes), f32),
+        out_shape=pltpu.VMEM((rows, 2 * chunks, lanes), f32),
         in_specs=[
             anywhere, anywhere, anywhere, anywhere, anywhere, anywhere, anywhere,
         ],

time: 27.3 us -> 24.8 us (0.908)
  Pallas kernels: 25.6 us -> 24 us
  local copies, waits for them, and re-layouts: 1.35 us -> 0.61 us
    pallas_call x1, Pallas kernels: 25.6 us -> 24 us  [one_kernel(): pl.pallas_call(functools.partial(fused, (n_sta, n_band), (tile, rows, pad...]
    unnamed x1, local copies, waits for them, and re-layouts: 1.35 us -> 0.61 us
where the time goes in v3:
time: 24.8 us; the launch traced here: 24.7 us
  Pallas kernels  24 us (97%)
  local copies, waits for them, and re-layouts  0.61 us (2%)
    pallas_call x1, Pallas kernels, one_kernel(): pl.pallas_call(functools.partial(fused, (n_sta, n_band), (tile, rows, pad...  24 us
    unnamed x1, local copies, waits for them, and re-layouts  0.61 us

profile of v3, /device:TPU:0, one launch (start us, length us, event | category | flops | bytes accessed | tf_op | source)
XLA Modules:
  0.0 24.7 jit_solution(14878536886771497081)
XLA Ops:
  0.0 24.0 %adjoint_kernel.1 = f32[6,8,128]{2,1,0:T(8,128)S(1)} custom-call(s32[1,2]{1,0:T(1,128)} %pair_hbm.1, s32[1,96]{1,0:T(1,128)} %bitcast.7, f32[4,2,128]{2,1,0:T(2,128)} %constant.6.clone.turn_hbm, f32[6,8,128]{2,1,0:T(8,128)} %bitcast.6, f32[2304,256]{1,0:T(8,128)} %bitcast.5, bf16[4,2,128,256]{3,2,1,0:T(8,128)(2,1)} %constant.7.clone.down_hbm, ...), custom_call_target="tpu_custom_call" | custom-call | tf_op jit(solution)/shard_map/adjoint_kernel/pallas_call | solution.py:453
  24.1 0.6 %copy.11 = f32[1,6,1024]{2,0,1:T(1,128)} copy(f32[1,6,1024]{2,0,1:T(1,128)S(1)} %bitcast.4) | data formatting | bytes 49152

commit v4 on v3

--- a/solution.py
+++ b/solution.py
@@ -352,11 +352,11 @@
         hooks = {}
         for c in range(1, chunks):
             if c > 1:
-                hooks.setdefault((c - 2) * tile + 28, []).append(functools.partial(relay, c))
-            hooks.setdefault((c - 1) * tile + 32, []).extend(
+                hooks.setdefault((c - 2) * tile + 16, []).append(functools.partial(relay, c))
+            hooks.setdefault((c - 1) * tile + 37, []).extend(
                 [functools.partial(choose, c), functools.partial(table, down, c - 1, 0)]
             )
-            hooks.setdefault((c - 1) * tile + 40, []).append(functools.partial(prepare, c))
+            hooks.setdefault((c - 1) * tile + 46, []).append(functools.partial(prepare, c))
         run(down_step, down_end, hooks)
 
         cols = [None] * 3
@@ -411,7 +411,7 @@
             at = (c + 1) * tile + delay
             hooks.setdefault(at, []).append(functools.partial(place, c))
             hooks.setdefault(at + 8, []).append(functools.partial(send, c))
-            hooks.setdefault(at + 80, []).append(functools.partial(combine, c))
+            hooks.setdefault(at + 64, []).append(functools.partial(combine, c))
         run(up_step, up_end, hooks)
 
     pl.run_scoped(

time: 24.8 us -> 24.4 us (0.984)
  Pallas kernels: 24 us -> 23.5 us
    pallas_call x1, Pallas kernels: 24 us -> 23.5 us  [one_kernel(): pl.pallas_call(functools.partial(fused, (n_sta, n_band), (tile, rows, pad...]
where the time goes in v4:
time: 24.4 us; the launch traced here: 24.2 us
  Pallas kernels  23.5 us (96%)
  local copies, waits for them, and re-layouts  0.61 us (2%)
    pallas_call x1, Pallas kernels, one_kernel(): pl.pallas_call(functools.partial(fused, (n_sta, n_band), (tile, rows, pad...  23.5 us
    unnamed x1, local copies, waits for them, and re-layouts  0.61 us

profile of v4, /device:TPU:0, one launch (start us, length us, event | category | flops | bytes accessed | tf_op | source)
XLA Modules:
  0.0 24.2 jit_solution(6701051654594872064)
XLA Ops:
  0.0 23.5 %adjoint_kernel.1 = f32[6,8,128]{2,1,0:T(8,128)S(1)} custom-call(s32[1,2]{1,0:T(1,128)} %pair_hbm.1, s32[1,96]{1,0:T(1,128)} %bitcast.7, f32[4,2,128]{2,1,0:T(2,128)} %constant.6.clone.turn_hbm, f32[6,8,128]{2,1,0:T(8,128)} %bitcast.6, f32[2304,256]{1,0:T(8,128)} %bitcast.5, bf16[4,2,128,256]{3,2,1,0:T(8,128)(2,1)} %constant.7.clone.down_hbm, ...), custom_call_target="tpu_custom_call" | custom-call | tf_op jit(solution)/shard_map/adjoint_kernel/pallas_call | solution.py:453
  23.5 0.6 %copy.11 = f32[1,6,1024]{2,0,1:T(1,128)} copy(f32[1,6,1024]{2,0,1:T(1,128)S(1)} %bitcast.4) | data formatting | bytes 49152

commit v5 on v4

--- a/solution.py
+++ b/solution.py
@@ -347,8 +347,8 @@
                     hook()
 
         choose(0)
+        relay(1)
         prepare(0)
-        relay(1)
         hooks = {}
         for c in range(1, chunks):
             if c > 1:

time: 24.4 us -> 24.4 us (level)
  no operation moved by 1% of the time
where the time goes in v5:
time: 24.4 us; the launch traced here: 24.2 us
  Pallas kernels  23.5 us (96%)
  local copies, waits for them, and re-layouts  0.61 us (2%)
    pallas_call x1, Pallas kernels, one_kernel(): pl.pallas_call(functools.partial(fused, (n_sta, n_band), (tile, rows, pad...  23.5 us
    unnamed x1, local copies, waits for them, and re-layouts  0.61 us

profile of v5, /device:TPU:0, one launch (start us, length us, event | category | flops | bytes accessed | tf_op | source)
XLA Modules:
  0.0 24.2 jit_solution(10586671226482105073)
XLA Ops:
  0.0 23.5 %adjoint_kernel.1 = f32[6,8,128]{2,1,0:T(8,128)S(1)} custom-call(s32[1,2]{1,0:T(1,128)} %pair_hbm.1, s32[1,96]{1,0:T(1,128)} %bitcast.7, f32[4,2,128]{2,1,0:T(2,128)} %constant.6.clone.turn_hbm, f32[6,8,128]{2,1,0:T(8,128)} %bitcast.6, f32[2304,256]{1,0:T(8,128)} %bitcast.5, bf16[4,2,128,256]{3,2,1,0:T(8,128)(2,1)} %constant.7.clone.down_hbm, ...), custom_call_target="tpu_custom_call" | custom-call | tf_op jit(solution)/shard_map/adjoint_kernel/pallas_call | solution.py:453
  23.6 0.6 %copy.11 = f32[1,6,1024]{2,0,1:T(1,128)} copy(f32[1,6,1024]{2,0,1:T(1,128)S(1)} %bitcast.4) | data formatting | bytes 49152
